TPU v7x, 32 devices: a whole 2x2x4 slice. The times are simulated.
32 devices in a mesh: line: 2 (over core), bus: 16 (over z, y, x).
Axes of the slice: x: 2, y: 2, z: 4, core: 2. Of those that a mesh axis runs over, the one named last changes fastest.
Arguments:
- injections: float32 [64, 69632], P(None, 'bus'), may hold values from -6 to 6
- transfer_factors: float32 [4096, 69632], P('line', 'bus'), may hold values from -0.0234375 to 0.0234375
- outage_factors: float32 [4096, 8192], P('line', 'bus'), may hold values from -1 to 1
- outage_line: int32 [8192], P('bus'), may hold values from 0 to 4095
- limit_table: int32 [4, 4096], P(None, 'line'), may hold values from 1 to 4
- scenario_tier: int32 [64], replicated, may hold values from 0 to 3
Outputs:
- injection_grad: float32 [64, 69632], P('line', 'bus')
- mean_penalty: float32 [64], replicated
All inputs are finite; a program needn't handle non-finite values.
Results may differ from a plain program's by a relative error of at most 0.0003.
Values sent between devices are 32-bit elements; how exact they have to be, the bound alone decides.
No kernel may reach another device: no remote copies, remote signals or barrier semaphores. Data moves between devices by JAX's collectives and lax.ppermute only.
A program may use at most 128 MiB of HBM per device.

v0:
```python
import functools

import jax
import jax.numpy as jnp
from jax import lax
from jax.experimental import pallas as pl
from jax.experimental.pallas import tpu as pltpu
from jax.sharding import PartitionSpec as P


SEND_LIMIT = 40
F32 = jnp.float32
BF16 = jnp.bfloat16
NT = (((1,), (1,)), ((), ()))
NN = (((1,), (0,)), ((), ()))


def split(x, parts):
    pieces = []
    for _ in range(parts):
        piece = x.astype(BF16)
        pieces.append(piece)
        x = x - piece.astype(F32)
    return pieces


def tile_of(extent, most):
    best = extent
    for size in range(128, most + 1, 128):
        if extent % size == 0:
            best = size
    return best


def tree_sum(values):
    values = list(values)
    while len(values) > 1:
        values = [values[i] + values[i + 1] for i in range(0, len(values), 2)]
    return values[0]


def flow_kernel(digits, fresh, index_ref, inj_ref, factor_ref, *rest):
    outs = rest[: len(digits)]
    if fresh:
        stacked, landed, arrived = rest[len(digits) :]
    else:
        stacked = inj_ref
        landed, arrived = rest[len(digits) :]
    count, tile, _ = landed.shape
    tiles = count // len(digits)

    def fetch(i, t):
        row = ((index_ref[0] ^ digits[i]) * tiles + t) * tile
        at = i * tiles + t
        return pltpu.make_async_copy(
            factor_ref.at[pl.ds(pl.multiple_of(row, tile), tile), :],
            landed.at[at],
            arrived.at[at],
        )

    for i in range(len(digits)):
        for t in range(tiles):
            fetch(i, t).start()
    scen = stacked.shape[0] // 2
    if fresh:
        high, low = split(inj_ref[...], 2)
        stacked[:scen, :] = high
        stacked[scen:, :] = low
    for i in range(len(digits)):

        def block(t, carry):
            fetch(i, t).wait()
            total = None
            for part in split(landed[i * tiles + t], 2):
                term = lax.dot_general(
                    part, stacked[...], NT, preferred_element_type=F32
                )
                total = term if total is None else total + term
            total = total.T
            at = pl.ds(pl.multiple_of(t * tile, tile), tile)
            outs[i][:, at] = total[:scen] + total[scen:]
            return carry

        lax.fori_loop(0, tiles, block, 0)


def partial_flows(injections, factors, group, digits, fresh, index, limit):
    rows, buses = factors.shape
    scen = injections.shape[0] if fresh else injections.shape[0] // 2
    block = rows // group
    tile = tile_of(block, 256)
    count = len(digits) * (block // tile)
    vmem = pl.BlockSpec(memory_space=pltpu.VMEM)
    stacked = [jax.ShapeDtypeStruct((2 * scen, buses), BF16)] if fresh else []
    return pl.pallas_call(
        functools.partial(flow_kernel, digits, fresh),
        in_specs=[
            pl.BlockSpec(memory_space=pltpu.SMEM),
            vmem,
            pl.BlockSpec(memory_space=pl.ANY),
        ],
        out_specs=[vmem] * (len(digits) + fresh),
        out_shape=[jax.ShapeDtypeStruct((scen, block), F32)] * len(digits) + stacked,
        scratch_shapes=[
            pltpu.VMEM((count, tile, buses), F32),
            pltpu.SemaphoreType.DMA((count,)),
        ],
        cost_estimate=pl.CostEstimate(
            flops=8 * scen * buses * count * tile,
            bytes_accessed=4 * buses * count * tile,
            transcendentals=0,
        ),
        name="partial_flows",
        compiler_params=pltpu.CompilerParams(vmem_limit_bytes=limit << 20),
    )(index, injections, factors)


def chosen(index_ref, j, block, outage_row):
    rows = lax.broadcasted_iota(jnp.int32, (block, outage_row.shape[1]), 0)
    start = index_ref[1] + (index_ref[0] ^ j) * block
    return jnp.where(rows + start == outage_row, 1.0, 0.0).astype(BF16)


def pick_kernel(group, index_ref, line_ref, *rest):
    flows, out = rest[:group], rest[group]
    scen, block = flows[0].shape
    total = None
    for j in range(group):
        lhs = jnp.concatenate(split(flows[j][...], 3), axis=0)
        part = lax.dot_general(
            lhs,
            chosen(index_ref, j, block, line_ref[...]),
            NN,
            preferred_element_type=F32,
        )
        part = part[:scen] + part[scen : 2 * scen] + part[2 * scen :]
        total = part if total is None else total + part
    out[...] = total


def carry_kernel(group, backs, scale, index_ref, line_ref, *rest):
    direct = rest[:group]
    parts = rest[group : group + backs]
    outs = rest[group + backs :]
    scen, block = direct[0].shape
    back = tree_sum([part[...] for part in parts])
    lhs = jnp.concatenate(split(back[:scen], 3), axis=0)
    for j in range(group):
        part = lax.dot_general(
            lhs,
            chosen(index_ref, j, block, line_ref[...]),
            NT,
            preferred_element_type=F32,
        )
        part = part[:scen] + part[scen : 2 * scen] + part[2 * scen :]
        outs[j][:scen, :] = scale * (direct[j][...] + part)
        outs[j][scen:, :] = back[scen:, :block]


def turn_kernel(group, index_ref, factor_ref, turned, energy, landed, arrived):
    lanes = 128
    _, outages, block = turned.shape

    def fetch(j):
        start = pl.multiple_of((index_ref[0] ^ j) * block, lanes)
        return pltpu.make_async_copy(
            factor_ref.at[pl.ds(start, block), :], landed.at[j], arrived.at[j]
        )

    for j in range(group):
        fetch(j).start()
    for j in range(group):
        fetch(j).wait()
        for k in range(outages // lanes):
            cut = slice(k * lanes, (k + 1) * lanes)
            squares = jnp.zeros((lanes, lanes), F32) if j == 0 else energy[cut, :]
            for c in range(block // lanes):
                place = slice(c * lanes, (c + 1) * lanes)
                part = landed[j, place, cut].T
                turned[j, cut, place] = part
                squares = squares + part * part
            energy[cut, :] = squares


def outage_kernel(group, others, index_ref, tier_ref, *rest):
    flows = rest[:group]
    picked = rest[group : group + others]
    turned, energy, table_ref, tiers_ref = rest[group + others : group + others + 4]
    rest = rest[group + others + 4 :]
    direct = rest[:group]
    back_ref = rest[group]
    level, all_picked, rows, wide, sums, held, held_back, pen, rows_pen, tier_rows = rest[
        group + 1 :
    ]
    scen, block = flows[0].shape
    outages = energy.shape[0]
    lanes = 128
    cols = block // lanes
    both = 2

    all_picked[...] = tree_sum([ref[...] for ref in picked])
    for j in range(group):
        start = pl.multiple_of((index_ref[0] ^ j) * block, lanes)
        level[j] = 0.4 * table_ref[:, pl.ds(start, block)].astype(F32)

    tiles = outages // lanes

    for k in range(tiles):
        rows[k] = all_picked[:, k * lanes : (k + 1) * lanes]

    def widen(r, s, k):
        at = pl.ds(pl.multiple_of(k * lanes, lanes), lanes)
        row = rows[k, pl.ds(s, 1), :]
        wide[r, at, :] = jnp.broadcast_to(row, (lanes, lanes)).T

    def fold(r, place, k):
        at = pl.ds(pl.multiple_of(k * lanes, lanes), lanes)
        to = pl.ds(pl.multiple_of(place * 8, 8), 8)
        turned_sums = sums[r, at, :].T
        held_back[k, to, :] = tree_sum(
            [turned_sums[8 * i : 8 * (i + 1)] for i in range(lanes // 8)]
        )

    tier_rows[...] = jnp.broadcast_to(tiers_ref[...].astype(F32), (lanes, scen)).T

    def pair(step, carry):
        losses = [None] * both
        for j in range(group):
            lows, highs, limits = [], [], []
            for r in range(both):
                s = step * both + r
                limit = level[j, pl.ds(tier_ref[s], 1), :]
                flow = flows[j][pl.ds(s, 1), :]
                low, high = -limit - flow, limit - flow
                for c in range(cols):
                    cut = slice(c * lanes, (c + 1) * lanes)
                    lows.append(jnp.broadcast_to(low[:, cut], (8, lanes)))
                    highs.append(jnp.broadcast_to(high[:, cut], (8, lanes)))
                    limits.append(limit[:, cut])

            def body(tile, state):
                state = list(state)
                if j == 0:
                    for r in range(both):
                        fold(r, step * both + r, tile)
                for k in range(lanes // 8):
                    at = pl.ds(pl.multiple_of(tile * lanes + k * 8, 8), 8)
                    factors = [
                        turned[j, at, c * lanes : (c + 1) * lanes] for c in range(cols)
                    ]
                    for r in range(both):
                        flow = wide[r, at, :]
                        total = flow * energy[at, :] if j == 0 else sums[r, at, :]
                        for c in range(cols):
                            n = r * cols + c
                            raised = jnp.maximum(factors[c] * flow, lows[n])
                            inside = jnp.minimum(raised, highs[n])
                            state[2 * n] = state[2 * n] + raised
                            state[2 * n + 1] = state[2 * n + 1] + inside
                            total = total - inside * factors[c]
                        sums[r, at, :] = total
                if j == group - 1:
                    later = jnp.minimum(step + 1, scen // both - 1)
                    for r in range(both):
                        widen(r, later * both + r, tile)
                return tuple(state)

            init = tuple([jnp.zeros((8, lanes), F32)] * (2 * both * cols))
            state = lax.fori_loop(0, tiles, body, init)
            for r in range(both):
                at = pl.ds(pl.multiple_of((step * both + r) * 8, 8), 8)
                for c in range(cols):
                    n = r * cols + c
                    raised, inside = state[2 * n], state[2 * n + 1]
                    held[j * cols + c, at, :] = inside
                    loss = limits[n] * (2.0 * raised - inside)
                    losses[r] = loss if losses[r] is None else losses[r] + loss
        for r in range(both):
            at = pl.ds(pl.multiple_of((step * both + r) * 8, 8), 8)
            pen[0, at, :] = losses[r]
        return carry

    sums[...] = jnp.zeros_like(sums)
    for r in range(both):
        for k in range(tiles):
            widen(r, r, k)
    lax.fori_loop(0, scen // both, pair, 0)
    for r in range(both):
        for k in range(tiles):
            fold(r, scen + r, k)

    for j in range(group):
        direct[j][...] = jnp.dot(
            all_picked[...],
            turned[j],
            precision=lax.Precision.HIGHEST,
            preferred_element_type=F32,
        )

    def gathered(ref, step, first, count, skip=0):
        base = (step * 8 + skip) * 8
        whole = [
            tree_sum([ref[i, pl.ds(base + r, 8, stride=8), :] for r in range(8)])
            for i in range(first, first + count)
        ]
        return jnp.concatenate(whole, axis=1)

    def finish(step, carry):
        at = pl.ds(pl.multiple_of(step * 8, 8), 8)
        back = gathered(held_back, step, 0, outages // lanes, both)
        back_ref[at, :] = back
        gain = jnp.sum(all_picked[at, :] * back, axis=1, keepdims=True)
        tiers = tier_rows[at, :1]
        for j in range(group):
            every = direct[j][at, :]
            here = every - gathered(held, step, j * cols, cols)
            limit = jnp.zeros_like(here)
            for t in range(table_ref.shape[0]):
                limit = jnp.where(tiers == t, level[j, t : t + 1, :], limit)
            direct[j][at, :] = here
            gain += jnp.sum(
                flows[j][at, :] * here + limit * every, axis=1, keepdims=True
            )
        loss = jnp.sum(gathered(pen, step, 0, 1), axis=1, keepdims=True)
        rows_pen[at, :] = jnp.broadcast_to(gain - loss, (8, lanes))
        return carry

    lax.fori_loop(0, scen // 8, finish, 0)
    back_ref[scen:, :] = jnp.zeros((back_ref.shape[0] - scen, outages), F32)
    back_ref[scen : scen + 1, :scen] = rows_pen[...].T[:1, :]


def spread_kernel(digits, lines, more, index_ref, *rest):
    grads = rest[: len(digits)]
    factor_ref = rest[len(digits)]
    rest = rest[len(digits) + 1 :]
    if more:
        begun_ref, rest = rest[0], rest[1:]
    outs, (stacked, landed, arrived) = rest[:-3], rest[-3:]
    scen, block = grads[0].shape
    rows = scen // lines
    steps, _, tile = landed.shape

    def fetch(step, i):
        row = pl.multiple_of((index_ref[0] ^ digits[i]) * block, 8)
        cut = pl.ds(pl.multiple_of(step * tile, tile), tile)
        return pltpu.make_async_copy(
            factor_ref.at[pl.ds(row, block), cut],
            landed.at[step, pl.ds(i * block, block), :],
            arrived.at[step, i],
        )

    for step in range(steps):
        for i in range(len(digits)):
            fetch(step, i).start()
    for j in range(len(digits)):
        for i in range(lines):
            at = pl.ds(pl.multiple_of((index_ref[1] ^ i) * rows, 8), rows)
            high, low = split(grads[j][at, :], 2)
            stacked[j, i * rows : (i + 1) * rows, :] = high.astype(F32)
            stacked[j, scen + i * rows : scen + (i + 1) * rows, :] = low.astype(F32)

    def piece(step, carry):
        cut = pl.ds(pl.multiple_of(step * tile, tile), tile)
        total = None
        for j in range(len(digits)):
            fetch(step, j).wait()
        for j in range(len(digits)):
            lhs = stacked[j].astype(BF16)
            for part in split(landed[step, j * block : (j + 1) * block, :], 2):
                term = lax.dot_general(lhs, part, NN, preferred_element_type=F32)
                total = term if total is None else total + term
        total = total[:scen] + total[scen:]
        if more:
            total = total + begun_ref[:, cut]
        count = scen // len(outs)
        for i in range(len(outs)):
            outs[i][:, cut] = total[i * count : (i + 1) * count]
        return carry

    lax.fori_loop(0, steps, piece, 0)


def spread(index, grads, digits, begun, factors, lines, limit):
    scen, block = grads[0].shape
    buses = factors.shape[1]
    tile = tile_of(buses, 256)
    steps = buses // tile
    more = begun is not None
    outs = lines if more else 1
    vmem = pl.BlockSpec(memory_space=pltpu.VMEM)
    return pl.pallas_call(
        functools.partial(spread_kernel, digits, lines, more),
        in_specs=[pl.BlockSpec(memory_space=pltpu.SMEM)]
        + [vmem] * len(grads)
        + [pl.BlockSpec(memory_space=pl.ANY)]
        + [vmem] * more,
        out_specs=[vmem] * outs,
        out_shape=[jax.ShapeDtypeStruct((scen // outs, buses), F32)] * outs,
        scratch_shapes=[
            pltpu.VMEM((len(grads), 2 * scen, block), F32),
            pltpu.VMEM((steps, len(grads) * block, tile), F32),
            pltpu.SemaphoreType.DMA((steps, len(grads))),
        ],
        cost_estimate=pl.CostEstimate(
            flops=8 * scen * buses * block * len(grads),
            bytes_accessed=4 * buses * block * len(grads),
            transcendentals=0,
        ),
        name="spread",
        compiler_params=pltpu.CompilerParams(vmem_limit_bytes=limit << 20),
    )(index, *grads, factors, *([begun] if more else []))


def exchange(values, axis, size, stride, count):
    got = [values[0]]
    for j in range(1, count):
        pairs = [(d, d ^ (j * stride)) for d in range(size)]
        got.append(lax.ppermute(values[j], axis, pairs))
    return got


def body(lines, buses, *args):
    return staged(lines, buses, *args)


def staged(lines, buses, injections, factors, outage_factors, outage_line, table, tier):
    scen = injections.shape[0]
    line_rows = factors.shape[0]
    outages = outage_factors.shape[1]
    group = min(4, buses)
    depth = buses // group
    block = line_rows // group
    bus = lax.axis_index("bus")
    line = lax.axis_index("line")
    local = jnp.stack([bus % group, line * line_rows]).astype(jnp.int32)
    order = jnp.stack([bus % group, line]).astype(jnp.int32)
    outage_row = outage_line.reshape(1, outages)
    smem = pl.BlockSpec(memory_space=pltpu.SMEM)
    vmem = pl.BlockSpec(memory_space=pltpu.VMEM)
    away = tuple(range(1, group))

    def reduce_all(pieces):
        mine = tree_sum(exchange(pieces, "bus", buses, 1, group))
        return tree_sum(exchange([mine] * depth, "bus", buses, group, depth))

    def gather_all(mine):
        return exchange([mine] * group, "bus", buses, 1, group)

    *sent, stacked = partial_flows(
        injections, factors, group, away, True, local, SEND_LIMIT
    )
    own = partial_flows(stacked, factors, group, (0,), False, local, 40)
    flows = gather_all(reduce_all([*own, *sent]))
    turned, energy = pl.pallas_call(
        functools.partial(turn_kernel, group),
        in_specs=[smem, pl.BlockSpec(memory_space=pl.ANY)],
        out_specs=[vmem] * 2,
        out_shape=[
            jax.ShapeDtypeStruct((group, outages, block), F32),
            jax.ShapeDtypeStruct((outages, 128), F32),
        ],
        scratch_shapes=[
            pltpu.VMEM((group, block, outages), F32),
            pltpu.SemaphoreType.DMA((group,)),
        ],
        cost_estimate=pl.CostEstimate(
            flops=2 * line_rows * outages,
            bytes_accessed=12 * line_rows * outages,
            transcendentals=0,
        ),
        name="turn",
        compiler_params=pltpu.CompilerParams(vmem_limit_bytes=6 << 20),
    )(local, outage_factors)
    picked = pl.pallas_call(
        functools.partial(pick_kernel, group),
        in_specs=[smem] + [vmem] * (group + 1),
        out_specs=vmem,
        out_shape=jax.ShapeDtypeStruct((scen, outages), F32),
        name="pick",
        compiler_params=pltpu.CompilerParams(vmem_limit_bytes=5 << 20),
    )(local, outage_row, *flows)
    picked = exchange([picked] * lines, "line", lines, 1, lines)
    results = pl.pallas_call(
        functools.partial(outage_kernel, group, lines),
        in_specs=[smem, smem] + [vmem] * (group + lines + 4),
        out_specs=[vmem] * (group + 1),
        out_shape=[jax.ShapeDtypeStruct((scen, block), F32)] * group
        + [jax.ShapeDtypeStruct((scen + 8, outages), F32)],
        scratch_shapes=[
            pltpu.VMEM((group, table.shape[0], block), F32),
            pltpu.VMEM((scen, outages), F32),
            pltpu.VMEM((outages // 128, scen, 128), F32),
            pltpu.VMEM((2, outages, 128), F32),
            pltpu.VMEM((2, outages, 128), F32),
            pltpu.VMEM((line_rows // 128, scen * 8, 128), F32),
            pltpu.VMEM((outages // 128, (scen + 2) * 8, 128), F32),
            pltpu.VMEM((1, scen * 8, 128), F32),
            pltpu.VMEM((scen, 128), F32),
            pltpu.VMEM((scen, 128), F32),
        ],
        name="outage_stage",
        compiler_params=pltpu.CompilerParams(vmem_limit_bytes=11 << 20),
    )(local, tier, *flows, *picked, turned, energy, table, tier.reshape(1, scen))
    direct, back = results[:group], results[group]
    backs = exchange([back] * lines, "line", lines, 1, lines)
    pieces = pl.pallas_call(
        functools.partial(carry_kernel, group, lines, 2.0 / (outages * buses)),
        in_specs=[smem] + [vmem] * (group + lines + 1),
        out_specs=[vmem] * group,
        out_shape=[jax.ShapeDtypeStruct((scen + 8, block), F32)] * group,
        name="carry",
        compiler_params=pltpu.CompilerParams(vmem_limit_bytes=5 << 20),
    )(local, outage_row, *direct, *backs)
    total = reduce_all(pieces)
    mean_penalty = total[scen, :scen] / (line_rows * lines * outages * buses)
    grads = gather_all(total[:scen])
    (begun,) = spread(order, grads[:1], (0,), None, factors, lines, 40)
    parts = spread(order, grads[1:], away, begun, factors, lines, 40)
    injection_grad = tree_sum(exchange(parts, "line", lines, 1, lines))
    return injection_grad, mean_penalty


def solution(mesh):
    buses = mesh.shape["bus"]
    return jax.shard_map(
        functools.partial(body, mesh.shape["line"], buses),
        mesh=mesh,
        in_specs=(
            P(None, "bus"),
            P("line", "bus"),
            P("line", "bus"),
            P("bus"),
            P(None, "line"),
            P(),
        ),
        out_specs=(P("line", "bus"), P()),
        check_vma=False,
    )
```

profile of v0, /device:TPU:0, one launch (start us, length us, event | category | flops | bytes accessed | tf_op | source)
XLA Modules:
  0.0 173.4 jit_solution(2344736737678295855)
XLA Ops:
  0.7 1.2 copy-done.1
  2.0 11.2 %partial_flows.2 = (f32[64,512]{1,0:T(8,128)S(1)}, f32[64,512]{1,0:T(8,128)S(1)}, f32[64,512]{1,0:T(8,128)S(1)}, bf16[128,4352]{1,0:T(8,128)(2,1)S(1)}) custom-call(s32[2]{0:T(128)S(1)} %pad_add_fusion.1.index_ref, f32[64,4352]{1,0:T(8,128)S(1)} %copy-done.1, f32[2048,4352]{1,0:T(8,128)} %rest_3_.1), custom_call_target="tpu_custom_call" | custom-call | flops 3422552064 | bytes 26738688 | tf_op jit(solution)/shard_map/partial_flows/pallas_call | solution.py:95
  13.2 3.0 %collective-permute-start = (f32[64,512]{1,0:T(8,128)S(1)}, f32[64,512]{1,0:T(8,128)S(1)}, u32[]{:S(2)}, u32[]{:S(2)}) collective-permute-start(f32[64,512]{1,0:T(8,128)S(1)} %get-tuple-element.20), channel_id=1, source_target_pairs={{0,1},{1,0},{2,3},{3,2},{4,5},{5,4},{6,7},{7,6},{8,9},{9,8},{10,11... | collective-permute-start | bytes 393224 | tf_op jit(solution)/shard_map/ppermute | solution.py:419
  16.2 1.5 collective-permute-start.1
  17.8 5.9 %partial_flows.3 = f32[64,512]{1,0:T(8,128)S(1)} custom-call(s32[2]{0:T(128)S(1)} %pad_add_fusion.1.index_ref, bf16[128,4352]{1,0:T(8,128)(2,1)S(1)} %get-tuple-element.19.inj_ref, f32[2048,4352]{1,0:T(8,128)} %rest_3_.1), custom_call_target="tpu_custom_call" | custom-call | flops 1140850688 | bytes 8912896 | tf_op jit(solution)/shard_map/partial_flows/pallas_call | solution.py:95
  24.1 3.9 %collective-permute-start.5 = (f32[64,512]{1,0:T(8,128)S(1)}, f32[64,512]{1,0:T(8,128)S(1)}, u32[]{:S(2)}, u32[]{:S(2)}) collective-permute-start(f32[64,512]{1,0:T(8,128)S(1)} %add_add_fusion.3), channel_id=1, source_target_pairs={{0,12},{1,13},{2,14},{3,15},{4,8},{5,9},{6,10},{7,11},{8,4},{9,5},... | collective-permute-start | bytes 393224 | tf_op jit(solution)/shard_map/ppermute | solution.py:419
  27.9 0.6 collective-permute-start.3
  28.6 3.7 %collective-permute-done.5 = f32[64,512]{1,0:T(8,128)S(1)} collective-permute-done((f32[64,512]{1,0:T(8,128)S(1)}, f32[64,512]{1,0:T(8,128)S(1)}, u32[]{:S(2)}, u32[]{:S(2)}) %collective-permute-start.5) | collective-permute-done | bytes 131104 | tf_op jit(solution)/shard_map/ppermute | solution.py:419
  32.3 5.9 %collective-permute-done.4 = f32[64,512]{1,0:T(8,128)S(1)} collective-permute-done((f32[64,512]{1,0:T(8,128)S(1)}, f32[64,512]{1,0:T(8,128)S(1)}, u32[]{:S(2)}, u32[]{:S(2)}) %collective-permute-start.4) | collective-permute-done | bytes 131104 | tf_op jit(solution)/shard_map/ppermute | solution.py:419
  38.2 2.5 %collective-permute-start.8 = (f32[64,512]{1,0:T(8,128)S(1)}, f32[64,512]{1,0:T(8,128)S(1)}, u32[]{:S(2)}, u32[]{:S(2)}) collective-permute-start(f32[64,512]{1,0:T(8,128)S(1)} %add_add_fusion.2.rest_0_), channel_id=1, source_target_pairs={{0,3},{1,2},{2,1},{3,0},{4,7},{5,6},{6,5},{7,4},{8,11},{9,10},{10,... | collective-permute-start | bytes 393224 | tf_op jit(solution)/shard_map/ppermute | solution.py:419
  41.8 3.1 %collective-permute-done.8.rest_3_ = f32[64,512]{1,0:T(8,128)S(1)} collective-permute-done((f32[64,512]{1,0:T(8,128)S(1)}, f32[64,512]{1,0:T(8,128)S(1)}, u32[]{:S(2)}, u32[]{:S(2)}) %collective-permute-start.8) | collective-permute-done | bytes 131104 | tf_op jit(solution)/shard_map/ppermute | solution.py:419
  44.9 1.7 collective-permute-done.7.rest_2_
  46.6 1.1 pick.1.rest_4_
  47.9 2.2 %turn.1 = (f32[4,512,512]{2,1,0:T(8,128)S(1)}, f32[512,128]{1,0:T(8,128)S(1)}) custom-call(s32[2]{0:T(128)S(1)} %pad_add_fusion.1.index_ref, f32[2048,512]{1,0:T(8,128)S(1)} %copy-done), custom_call_target="tpu_custom_call" | custom-call | flops 2097152 | bytes 12582912 | tf_op jit(solution)/shard_map/turn/pallas_call | solution.py:455
  50.1 73.6 %outage_stage.1 = (f32[64,512]{1,0:T(8,128)S(1)}, f32[64,512]{1,0:T(8,128)S(1)}, f32[64,512]{1,0:T(8,128)S(1)}, f32[64,512]{1,0:T(8,128)S(1)}, f32[72,512]{1,0:T(8,128)S(1)}) custom-call(s32[2]{0:T(128)S(1)} %pad_add_fusion.1.index_ref, s32[64]{0:T(128)S(1)} %copy-done.4, f32[64,512]{1,0:T(8,128)S(1)} %add_add_fusion.2.rest_0_, ...), custom_call_target="tpu_custom_call" | custom-call | tf_op jit(solution)/shard_map/outage_stage/pallas_call | solution.py:484
  124.3 1.0 collective-permute-done.10.rest_5_
  125.3 1.4 carry.1
  126.7 1.6 collective-permute-start.11
  128.3 0.7 collective-permute-start.12
  129.0 1.3 collective-permute-start.13
  130.3 3.2 %collective-permute-done.11 = f32[72,512]{1,0:T(8,128)S(1)} collective-permute-done((f32[72,512]{1,0:T(8,128)S(1)}, f32[72,512]{1,0:T(8,128)S(1)}, u32[]{:S(2)}, u32[]{:S(2)}) %collective-permute-start.11) | collective-permute-done | bytes 147488 | tf_op jit(solution)/shard_map/ppermute | solution.py:419
  133.5 3.8 %collective-permute-done.12 = f32[72,512]{1,0:T(8,128)S(1)} collective-permute-done((f32[72,512]{1,0:T(8,128)S(1)}, f32[72,512]{1,0:T(8,128)S(1)}, u32[]{:S(2)}, u32[]{:S(2)}) %collective-permute-start.12) | collective-permute-done | bytes 147488 | tf_op jit(solution)/shard_map/ppermute | solution.py:419
  137.3 1.8 %collective-permute-start.16 = (f32[72,512]{1,0:T(8,128)S(1)}, f32[72,512]{1,0:T(8,128)S(1)}, u32[]{:S(2)}, u32[]{:S(2)}) collective-permute-start(f32[72,512]{1,0:T(8,128)S(1)} %add_add_fusion.1), channel_id=1, source_target_pairs={{0,12},{1,13},{2,14},{3,15},{4,8},{5,9},{6,10},{7,11},{8,4},{9,5},... | collective-permute-start | bytes 442376 | tf_op jit(solution)/shard_map/ppermute | solution.py:419
  139.2 2.6 %collective-permute-start.14 = (f32[72,512]{1,0:T(8,128)S(1)}, f32[72,512]{1,0:T(8,128)S(1)}, u32[]{:S(2)}, u32[]{:S(2)}) collective-permute-start(f32[72,512]{1,0:T(8,128)S(1)} %add_add_fusion.1), channel_id=1, source_target_pairs={{0,4},{1,5},{2,6},{3,7},{4,0},{5,1},{6,2},{7,3},{8,12},{9,13},{10,... | collective-permute-start | bytes 442376 | tf_op jit(solution)/shard_map/ppermute | solution.py:419
  141.8 4.1 %collective-permute-done.16 = f32[72,512]{1,0:T(8,128)S(1)} collective-permute-done((f32[72,512]{1,0:T(8,128)S(1)}, f32[72,512]{1,0:T(8,128)S(1)}, u32[]{:S(2)}, u32[]{:S(2)}) %collective-permute-start.16) | collective-permute-done | bytes 147488 | tf_op jit(solution)/shard_map/ppermute | solution.py:419
  145.9 4.8 %collective-permute-done.15 = f32[72,512]{1,0:T(8,128)S(1)} collective-permute-done((f32[72,512]{1,0:T(8,128)S(1)}, f32[72,512]{1,0:T(8,128)S(1)}, u32[]{:S(2)}, u32[]{:S(2)}) %collective-permute-start.15) | collective-permute-done | bytes 147488 | tf_op jit(solution)/shard_map/ppermute | solution.py:419
  150.7 1.7 collective-permute-start.19
  153.1 1.2 collective-permute-start.17
  154.4 5.8 %spread.2.rest_4_ = f32[64,4352]{1,0:T(8,128)S(1)} custom-call(s32[2]{0:T(128)S(1)} %pad_add_fusion.index_ref, f32[64,512]{1,0:T(8,128)S(1)} %slice.8.rest_0_, f32[2048,4352]{1,0:T(8,128)} %rest_3_.1), custom_call_target="tpu_custom_call" | custom-call | flops 1140850688 | bytes 8912896 | tf_op jit(solution)/shard_map/spread/pallas_call | solution.py:392
  160.2 10.2 %spread.3 = (f32[32,4352]{1,0:T(8,128)S(1)}, f32[32,4352]{1,0:T(8,128)S(1)}) custom-call(s32[2]{0:T(128)S(1)} %pad_add_fusion.index_ref, f32[64,512]{1,0:T(8,128)S(1)} %collective-permute-done.17.rest_0_, f32[64,512]{1,0:T(8,128)S(1)} %collective-permute-done.18.rest_1_, f32[64,512]{1,0:T(8,128)S(1)} %collective-permute-done.19.rest_2_, ...), custom_call_target="tpu_custom_call" | custom-call | flops 3422552064 | bytes 26738688 | tf_op jit(solution)/shard_map/spread/pallas_call | solution.py:392
  171.0 1.4 collective-permute-done.20
  172.5 0.9 add.57
  (37 shorter events, 3.6 us)
Async XLA Ops:
  0.7 1.2 copy-start.1
  13.2 10.5 %collective-permute-start = (f32[64,512]{1,0:T(8,128)S(1)}, f32[64,512]{1,0:T(8,128)S(1)}, u32[]{:S(2)}, u32[]{:S(2)}) collective-permute-start(f32[64,512]{1,0:T(8,128)S(1)} %get-tuple-element.20), channel_id=1, source_target_pairs={{0,1},{1,0},{2,3},{3,2},{4,5},{5,4},{6,7},{7,6},{8,9},{9,8},{10,11... | collective-permute-start | bytes 393224 | tf_op jit(solution)/shard_map/ppermute | solution.py:419
  16.2 7.8 %collective-permute-start.1 = (f32[64,512]{1,0:T(8,128)S(1)}, f32[64,512]{1,0:T(8,128)S(1)}, u32[]{:S(2)}, u32[]{:S(2)}) collective-permute-start(f32[64,512]{1,0:T(8,128)S(1)} %get-tuple-element.21), channel_id=1, source_target_pairs={{0,2},{1,3},{2,0},{3,1},{4,6},{5,7},{6,4},{7,5},{8,10},{9,11},{10,... | collective-permute-start | bytes 393224 | tf_op jit(solution)/shard_map/ppermute | solution.py:419
  17.8 6.3 %collective-permute-start.2 = (f32[64,512]{1,0:T(8,128)S(1)}, f32[64,512]{1,0:T(8,128)S(1)}, u32[]{:S(2)}, u32[]{:S(2)}) collective-permute-start(f32[64,512]{1,0:T(8,128)S(1)} %get-tuple-element.22), channel_id=1, source_target_pairs={{0,3},{1,2},{2,1},{3,0},{4,7},{5,6},{6,5},{7,4},{8,11},{9,10},{10,... | collective-permute-start | bytes 393224 | tf_op jit(solution)/shard_map/ppermute | solution.py:419
  17.8 28.9 %copy-start.3 = (s32[512]{0:T(512)S(1)}, s32[512]{0:T(512)}, u32[]{:S(2)}) copy-start(s32[512]{0:T(512)} %param.9) | copy-start | bytes 6148
  17.8 30.1 %copy-start = (f32[2048,512]{1,0:T(8,128)S(1)}, f32[2048,512]{1,0:T(8,128)}, u32[]{:S(2)}) copy-start(f32[2048,512]{1,0:T(8,128)} %factor_ref.5) | copy-start | bytes 12582916
  23.7 26.4 %copy-start.2 = (s32[4,2048]{1,0:T(4,128)S(1)}, s32[4,2048]{1,0:T(4,128)}, u32[]{:S(2)}) copy-start(s32[4,2048]{1,0:T(4,128)} %rest_8_.1) | copy-start | bytes 98308
  23.7 26.4 %copy-start.4 = (s32[64]{0:T(128)S(1)}, s32[64]{0:T(128)}, u32[]{:S(2)}) copy-start(s32[64]{0:T(128)} %tier_ref.1) | copy-start | bytes 772
  24.1 8.2 %collective-permute-start.5 = (f32[64,512]{1,0:T(8,128)S(1)}, f32[64,512]{1,0:T(8,128)S(1)}, u32[]{:S(2)}, u32[]{:S(2)}) collective-permute-start(f32[64,512]{1,0:T(8,128)S(1)} %add_add_fusion.3), channel_id=1, source_target_pairs={{0,12},{1,13},{2,14},{3,15},{4,8},{5,9},{6,10},{7,11},{8,4},{9,5},... | collective-permute-start | bytes 393224 | tf_op jit(solution)/shard_map/ppermute | solution.py:419
  27.9 10.2 %collective-permute-start.4 = (f32[64,512]{1,0:T(8,128)S(1)}, f32[64,512]{1,0:T(8,128)S(1)}, u32[]{:S(2)}, u32[]{:S(2)}) collective-permute-start(f32[64,512]{1,0:T(8,128)S(1)} %add_add_fusion.3), channel_id=1, source_target_pairs={{0,8},{1,9},{2,10},{3,11},{4,12},{5,13},{6,14},{7,15},{8,0},{9,1},... | collective-permute-start | bytes 393224 | tf_op jit(solution)/shard_map/ppermute | solution.py:419
  27.9 10.2 %collective-permute-start.3 = (f32[64,512]{1,0:T(8,128)S(1)}, f32[64,512]{1,0:T(8,128)S(1)}, u32[]{:S(2)}, u32[]{:S(2)}) collective-permute-start(f32[64,512]{1,0:T(8,128)S(1)} %add_add_fusion.3), channel_id=1, source_target_pairs={{0,4},{1,5},{2,6},{3,7},{4,0},{5,1},{6,2},{7,3},{8,12},{9,13},{10,... | collective-permute-start | bytes 393224 | tf_op jit(solution)/shard_map/ppermute | solution.py:419
  38.2 6.7 %collective-permute-start.8 = (f32[64,512]{1,0:T(8,128)S(1)}, f32[64,512]{1,0:T(8,128)S(1)}, u32[]{:S(2)}, u32[]{:S(2)}) collective-permute-start(f32[64,512]{1,0:T(8,128)S(1)} %add_add_fusion.2.rest_0_), channel_id=1, source_target_pairs={{0,3},{1,2},{2,1},{3,0},{4,7},{5,6},{6,5},{7,4},{8,11},{9,10},{10,... | collective-permute-start | bytes 393224 | tf_op jit(solution)/shard_map/ppermute | solution.py:419
  40.7 5.8 %collective-permute-start.7 = (f32[64,512]{1,0:T(8,128)S(1)}, f32[64,512]{1,0:T(8,128)S(1)}, u32[]{:S(2)}, u32[]{:S(2)}) collective-permute-start(f32[64,512]{1,0:T(8,128)S(1)} %add_add_fusion.2.rest_0_), channel_id=1, source_target_pairs={{0,2},{1,3},{2,0},{3,1},{4,6},{5,7},{6,4},{7,5},{8,10},{9,11},{10,... | collective-permute-start | bytes 393224 | tf_op jit(solution)/shard_map/ppermute | solution.py:419
  41.2 5.4 %collective-permute-start.6 = (f32[64,512]{1,0:T(8,128)S(1)}, f32[64,512]{1,0:T(8,128)S(1)}, u32[]{:S(2)}, u32[]{:S(2)}) collective-permute-start(f32[64,512]{1,0:T(8,128)S(1)} %add_add_fusion.2.rest_0_), channel_id=1, source_target_pairs={{0,1},{1,0},{2,3},{3,2},{4,5},{5,4},{6,7},{7,6},{8,9},{9,8},{10,11... | collective-permute-start | bytes 393224 | tf_op jit(solution)/shard_map/ppermute | solution.py:419
  47.8 2.3 %collective-permute-start.9 = (f32[64,512]{1,0:T(8,128)S(1)}, f32[64,512]{1,0:T(8,128)S(1)}, u32[]{:S(2)}, u32[]{:S(2)}) collective-permute-start(f32[64,512]{1,0:T(8,128)S(1)} %pick.1.rest_4_), channel_id=1, source_target_pairs={{0,16},{16,0},{1,17},{17,1},{2,18},{18,2},{3,19},{19,3},{4,20},{20... | collective-permute-start | bytes 393224 | tf_op jit(solution)/shard_map/ppermute | solution.py:419
  123.8 1.5 collective-permute-start.10
  126.7 6.8 %collective-permute-start.11 = (f32[72,512]{1,0:T(8,128)S(1)}, f32[72,512]{1,0:T(8,128)S(1)}, u32[]{:S(2)}, u32[]{:S(2)}) collective-permute-start(f32[72,512]{1,0:T(8,128)S(1)} %get-tuple-element.31), channel_id=1, source_target_pairs={{0,1},{1,0},{2,3},{3,2},{4,5},{5,4},{6,7},{7,6},{8,9},{9,8},{10,11... | collective-permute-start | bytes 442376 | tf_op jit(solution)/shard_map/ppermute | solution.py:419
  128.3 9.0 %collective-permute-start.12 = (f32[72,512]{1,0:T(8,128)S(1)}, f32[72,512]{1,0:T(8,128)S(1)}, u32[]{:S(2)}, u32[]{:S(2)}) collective-permute-start(f32[72,512]{1,0:T(8,128)S(1)} %get-tuple-element.32), channel_id=1, source_target_pairs={{0,2},{1,3},{2,0},{3,1},{4,6},{5,7},{6,4},{7,5},{8,10},{9,11},{10,... | collective-permute-start | bytes 442376 | tf_op jit(solution)/shard_map/ppermute | solution.py:419
  129.0 8.3 %collective-permute-start.13 = (f32[72,512]{1,0:T(8,128)S(1)}, f32[72,512]{1,0:T(8,128)S(1)}, u32[]{:S(2)}, u32[]{:S(2)}) collective-permute-start(f32[72,512]{1,0:T(8,128)S(1)} %get-tuple-element.33), channel_id=1, source_target_pairs={{0,3},{1,2},{2,1},{3,0},{4,7},{5,6},{6,5},{7,4},{8,11},{9,10},{10,... | collective-permute-start | bytes 442376 | tf_op jit(solution)/shard_map/ppermute | solution.py:419
  137.3 8.6 %collective-permute-start.16 = (f32[72,512]{1,0:T(8,128)S(1)}, f32[72,512]{1,0:T(8,128)S(1)}, u32[]{:S(2)}, u32[]{:S(2)}) collective-permute-start(f32[72,512]{1,0:T(8,128)S(1)} %add_add_fusion.1), channel_id=1, source_target_pairs={{0,12},{1,13},{2,14},{3,15},{4,8},{5,9},{6,10},{7,11},{8,4},{9,5},... | collective-permute-start | bytes 442376 | tf_op jit(solution)/shard_map/ppermute | solution.py:419
  139.2 11.5 %collective-permute-start.15 = (f32[72,512]{1,0:T(8,128)S(1)}, f32[72,512]{1,0:T(8,128)S(1)}, u32[]{:S(2)}, u32[]{:S(2)}) collective-permute-start(f32[72,512]{1,0:T(8,128)S(1)} %add_add_fusion.1), channel_id=1, source_target_pairs={{0,8},{1,9},{2,10},{3,11},{4,12},{5,13},{6,14},{7,15},{8,0},{9,1},... | collective-permute-start | bytes 442376 | tf_op jit(solution)/shard_map/ppermute | solution.py:419
  139.2 11.5 %collective-permute-start.14 = (f32[72,512]{1,0:T(8,128)S(1)}, f32[72,512]{1,0:T(8,128)S(1)}, u32[]{:S(2)}, u32[]{:S(2)}) collective-permute-start(f32[72,512]{1,0:T(8,128)S(1)} %add_add_fusion.1), channel_id=1, source_target_pairs={{0,4},{1,5},{2,6},{3,7},{4,0},{5,1},{6,2},{7,3},{8,12},{9,13},{10,... | collective-permute-start | bytes 442376 | tf_op jit(solution)/shard_map/ppermute | solution.py:419
  150.7 9.4 %collective-permute-start.19 = (f32[64,512]{1,0:T(8,128)S(1)}, f32[64,512]{1,0:T(8,128)S(1)}, u32[]{:S(2)}, u32[]{:S(2)}) collective-permute-start(f32[64,512]{1,0:T(8,128)S(1)} %slice.8.rest_0_), channel_id=1, source_target_pairs={{0,3},{1,2},{2,1},{3,0},{4,7},{5,6},{6,5},{7,4},{8,11},{9,10},{10,... | collective-permute-start | bytes 393224 | tf_op jit(solution)/shard_map/ppermute | solution.py:419
  152.4 7.7 %collective-permute-start.18 = (f32[64,512]{1,0:T(8,128)S(1)}, f32[64,512]{1,0:T(8,128)S(1)}, u32[]{:S(2)}, u32[]{:S(2)}) collective-permute-start(f32[64,512]{1,0:T(8,128)S(1)} %slice.8.rest_0_), channel_id=1, source_target_pairs={{0,2},{1,3},{2,0},{3,1},{4,6},{5,7},{6,4},{7,5},{8,10},{9,11},{10,... | collective-permute-start | bytes 393224 | tf_op jit(solution)/shard_map/ppermute | solution.py:419
  153.1 7.1 %collective-permute-start.17 = (f32[64,512]{1,0:T(8,128)S(1)}, f32[64,512]{1,0:T(8,128)S(1)}, u32[]{:S(2)}, u32[]{:S(2)}) collective-permute-start(f32[64,512]{1,0:T(8,128)S(1)} %slice.8.rest_0_), channel_id=1, source_target_pairs={{0,1},{1,0},{2,3},{3,2},{4,5},{5,4},{6,7},{7,6},{8,9},{9,8},{10,11... | collective-permute-start | bytes 393224 | tf_op jit(solution)/shard_map/ppermute | solution.py:419
  170.5 2.0 %collective-permute-start.20 = (f32[32,4352]{1,0:T(8,128)S(1)}, f32[32,4352]{1,0:T(8,128)S(1)}, u32[]{:S(2)}, u32[]{:S(2)}) collective-permute-start(f32[32,4352]{1,0:T(8,128)S(1)} %get-tuple-element.35), channel_id=1, source_target_pairs={{0,16},{16,0},{1,17},{17,1},{2,18},{18,2},{3,19},{19,3},{4,20},{20... | collective-permute-start | bytes 1671176 | tf_op jit(solution)/shard_map/ppermute | solution.py:419
where the time goes:
time: 174 us; the launch traced here: 173 us
  Pallas kernels  112 us (64%)
  waiting for transfers between devices  33.1 us (19%)
  starting transfers between devices  24.8 us (14%)
    pallas_call x1, Pallas kernels, staged(): pl.pallas_call(functools.partial(outage_kernel, group, lines), in_specs=[...  73.6 us
    ppermute x21, waiting for transfers between devices, exchange(): got.append(lax.ppermute(values[j], axis, pairs))  33.1 us
    ppermute x21, starting transfers between devices, exchange(): got.append(lax.ppermute(values[j], axis, pairs))  24.8 us
    pallas_call x2, Pallas kernels, partial_flows(): pl.pallas_call(functools.partial(flow_kernel, digits, fresh), in_specs=[p...  17.1 us
    pallas_call x2, Pallas kernels, spread(): pl.pallas_call(functools.partial(spread_kernel, digits, lines, more), in_...  16 us
  transfers between devices with their start and end apart: 21, of which 12 were waited for; matrix products, arithmetic and copies ran while one was open for 0% of the time, Pallas kernels for 8%

commit v1 on v0

--- a/solution.py
+++ b/solution.py
@@ -13,6 +13,10 @@
 BF16 = jnp.bfloat16
 NT = (((1,), (1,)), ((), ()))
 NN = (((1,), (0,)), ((), ()))
+
+
+def near(group):
+    return lax.rem(lax.axis_index("bus"), group)
 
 
 def split(x, parts):
@@ -39,10 +43,12 @@
     return values[0]
 
 
-def flow_kernel(digits, fresh, index_ref, inj_ref, factor_ref, *rest):
+def flow_kernel(group, digits, fresh, inj_ref, factor_ref, *rest):
     outs = rest[: len(digits)]
     if fresh:
-        stacked, landed, arrived = rest[len(digits) :]
+        stacked, landed, arrived, raw, ready = rest[len(digits) :]
+        first = pltpu.make_async_copy(inj_ref, raw, ready)
+        first.start()
     else:
         stacked = inj_ref
         landed, arrived = rest[len(digits) :]
@@ -50,7 +56,7 @@
     tiles = count // len(digits)
 
     def fetch(i, t):
-        row = ((index_ref[0] ^ digits[i]) * tiles + t) * tile
+        row = ((near(group) ^ digits[i]) * tiles + t) * tile
         at = i * tiles + t
         return pltpu.make_async_copy(
             factor_ref.at[pl.ds(pl.multiple_of(row, tile), tile), :],
@@ -63,7 +69,8 @@
             fetch(i, t).start()
     scen = stacked.shape[0] // 2
     if fresh:
-        high, low = split(inj_ref[...], 2)
+        first.wait()
+        high, low = split(raw[...], 2)
         stacked[:scen, :] = high
         stacked[scen:, :] = low
     for i in range(len(digits)):
@@ -84,7 +91,7 @@
         lax.fori_loop(0, tiles, block, 0)
 
 
-def partial_flows(injections, factors, group, digits, fresh, index, limit):
+def partial_flows(injections, factors, group, digits, fresh, limit):
     rows, buses = factors.shape
     scen = injections.shape[0] if fresh else injections.shape[0] // 2
     block = rows // group
@@ -93,10 +100,9 @@
     vmem = pl.BlockSpec(memory_space=pltpu.VMEM)
     stacked = [jax.ShapeDtypeStruct((2 * scen, buses), BF16)] if fresh else []
     return pl.pallas_call(
-        functools.partial(flow_kernel, digits, fresh),
+        functools.partial(flow_kernel, group, digits, fresh),
         in_specs=[
-            pl.BlockSpec(memory_space=pltpu.SMEM),
-            vmem,
+            pl.BlockSpec(memory_space=pl.ANY) if fresh else vmem,
             pl.BlockSpec(memory_space=pl.ANY),
         ],
         out_specs=[vmem] * (len(digits) + fresh),
@@ -104,7 +110,8 @@
         scratch_shapes=[
             pltpu.VMEM((count, tile, buses), F32),
             pltpu.SemaphoreType.DMA((count,)),
-        ],
+        ]
+        + [pltpu.VMEM((scen, buses), F32), pltpu.SemaphoreType.DMA] * fresh,
         cost_estimate=pl.CostEstimate(
             flops=8 * scen * buses * count * tile,
             bytes_accessed=4 * buses * count * tile,
@@ -112,16 +119,16 @@
         ),
         name="partial_flows",
         compiler_params=pltpu.CompilerParams(vmem_limit_bytes=limit << 20),
-    )(index, injections, factors)
-
-
-def chosen(index_ref, j, block, outage_row):
+    )(injections, factors)
+
+
+def chosen(group, j, block, outage_row):
     rows = lax.broadcasted_iota(jnp.int32, (block, outage_row.shape[1]), 0)
-    start = index_ref[1] + (index_ref[0] ^ j) * block
+    start = (lax.axis_index("line") * group + (near(group) ^ j)) * block
     return jnp.where(rows + start == outage_row, 1.0, 0.0).astype(BF16)
 
 
-def pick_kernel(group, index_ref, line_ref, *rest):
+def pick_kernel(group, line_ref, *rest):
     flows, out = rest[:group], rest[group]
     scen, block = flows[0].shape
     total = None
@@ -129,7 +136,7 @@
         lhs = jnp.concatenate(split(flows[j][...], 3), axis=0)
         part = lax.dot_general(
             lhs,
-            chosen(index_ref, j, block, line_ref[...]),
+            chosen(group, j, block, line_ref[...]),
             NN,
             preferred_element_type=F32,
         )
@@ -138,7 +145,7 @@
     out[...] = total
 
 
-def carry_kernel(group, backs, scale, index_ref, line_ref, *rest):
+def carry_kernel(group, backs, scale, line_ref, *rest):
     direct = rest[:group]
     parts = rest[group : group + backs]
     outs = rest[group + backs :]
@@ -148,7 +155,7 @@
     for j in range(group):
         part = lax.dot_general(
             lhs,
-            chosen(index_ref, j, block, line_ref[...]),
+            chosen(group, j, block, line_ref[...]),
             NT,
             preferred_element_type=F32,
         )
@@ -157,12 +164,12 @@
         outs[j][scen:, :] = back[scen:, :block]
 
 
-def turn_kernel(group, index_ref, factor_ref, turned, energy, landed, arrived):
+def turn_kernel(group, factor_ref, turned, energy, terms, landed, arrived):
     lanes = 128
     _, outages, block = turned.shape
 
     def fetch(j):
-        start = pl.multiple_of((index_ref[0] ^ j) * block, lanes)
+        start = pl.multiple_of((near(group) ^ j) * block, lanes)
         return pltpu.make_async_copy(
             factor_ref.at[pl.ds(start, block), :], landed.at[j], arrived.at[j]
         )
@@ -179,14 +186,16 @@
                 part = landed[j, place, cut].T
                 turned[j, cut, place] = part
                 squares = squares + part * part
+                for n, term in enumerate(split(part, 3)):
+                    terms[n, j, cut, place] = term
             energy[cut, :] = squares
 
 
-def outage_kernel(group, others, index_ref, tier_ref, *rest):
+def outage_kernel(group, others, tier_ref, *rest):
     flows = rest[:group]
     picked = rest[group : group + others]
-    turned, energy, table_ref, tiers_ref = rest[group + others : group + others + 4]
-    rest = rest[group + others + 4 :]
+    turned, energy, terms, table_ref, tiers_ref = rest[group + others :][:5]
+    rest = rest[group + others + 5 :]
     direct = rest[:group]
     back_ref = rest[group]
     level, all_picked, rows, wide, sums, held, held_back, pen, rows_pen, tier_rows = rest[
@@ -200,7 +209,7 @@
 
     all_picked[...] = tree_sum([ref[...] for ref in picked])
     for j in range(group):
-        start = pl.multiple_of((index_ref[0] ^ j) * block, lanes)
+        start = pl.multiple_of((near(group) ^ j) * block, lanes)
         level[j] = 0.4 * table_ref[:, pl.ds(start, block)].astype(F32)
 
     tiles = outages // lanes
@@ -238,13 +247,16 @@
                     highs.append(jnp.broadcast_to(high[:, cut], (8, lanes)))
                     limits.append(limit[:, cut])
 
+            wide_trip = 0 < j < group - 1 and tiles % 2 == 0
+            length = 2 * lanes if wide_trip else lanes
+
             def body(tile, state):
                 state = list(state)
                 if j == 0:
                     for r in range(both):
                         fold(r, step * both + r, tile)
-                for k in range(lanes // 8):
-                    at = pl.ds(pl.multiple_of(tile * lanes + k * 8, 8), 8)
+                for k in range(length // 8):
+                    at = pl.ds(pl.multiple_of(tile * length + k * 8, 8), 8)
                     factors = [
                         turned[j, at, c * lanes : (c + 1) * lanes] for c in range(cols)
                     ]
@@ -266,7 +278,7 @@
                 return tuple(state)
 
             init = tuple([jnp.zeros((8, lanes), F32)] * (2 * both * cols))
-            state = lax.fori_loop(0, tiles, body, init)
+            state = lax.fori_loop(0, outages // length, body, init)
             for r in range(both):
                 at = pl.ds(pl.multiple_of((step * both + r) * 8, 8), 8)
                 for c in range(cols):
@@ -289,13 +301,18 @@
         for k in range(tiles):
             fold(r, scen + r, k)
 
+    split_picked = split(all_picked[...], 3)
     for j in range(group):
-        direct[j][...] = jnp.dot(
-            all_picked[...],
-            turned[j],
-            precision=lax.Precision.HIGHEST,
-            preferred_element_type=F32,
-        )
+        every = None
+        for n in (2, 1, 0):
+            lhs = jnp.concatenate(split_picked[: 3 - n], axis=0)
+            part = lax.dot_general(
+                lhs, terms[n, j], NN, preferred_element_type=F32
+            )
+            for i in reversed(range(3 - n)):
+                piece = part[i * scen : (i + 1) * scen]
+                every = piece if every is None else every + piece
+        direct[j][...] = every
 
     def gathered(ref, step, first, count, skip=0):
         base = (step * 8 + skip) * 8
@@ -330,7 +347,7 @@
     back_ref[scen : scen + 1, :scen] = rows_pen[...].T[:1, :]
 
 
-def spread_kernel(digits, lines, more, index_ref, *rest):
+def spread_kernel(group, digits, lines, more, *rest):
     grads = rest[: len(digits)]
     factor_ref = rest[len(digits)]
     rest = rest[len(digits) + 1 :]
@@ -342,7 +359,7 @@
     steps, _, tile = landed.shape
 
     def fetch(step, i):
-        row = pl.multiple_of((index_ref[0] ^ digits[i]) * block, 8)
+        row = pl.multiple_of((near(group) ^ digits[i]) * block, 8)
         cut = pl.ds(pl.multiple_of(step * tile, tile), tile)
         return pltpu.make_async_copy(
             factor_ref.at[pl.ds(row, block), cut],
@@ -355,7 +372,8 @@
             fetch(step, i).start()
     for j in range(len(digits)):
         for i in range(lines):
-            at = pl.ds(pl.multiple_of((index_ref[1] ^ i) * rows, 8), rows)
+            place = (lax.axis_index("line") ^ i) * rows
+            at = pl.ds(pl.multiple_of(place, 8), rows)
             high, low = split(grads[j][at, :], 2)
             stacked[j, i * rows : (i + 1) * rows, :] = high.astype(F32)
             stacked[j, scen + i * rows : scen + (i + 1) * rows, :] = low.astype(F32)
@@ -381,7 +399,7 @@
     lax.fori_loop(0, steps, piece, 0)
 
 
-def spread(index, grads, digits, begun, factors, lines, limit):
+def spread(group, grads, digits, begun, factors, lines, limit):
     scen, block = grads[0].shape
     buses = factors.shape[1]
     tile = tile_of(buses, 256)
@@ -390,9 +408,8 @@
     outs = lines if more else 1
     vmem = pl.BlockSpec(memory_space=pltpu.VMEM)
     return pl.pallas_call(
-        functools.partial(spread_kernel, digits, lines, more),
-        in_specs=[pl.BlockSpec(memory_space=pltpu.SMEM)]
-        + [vmem] * len(grads)
+        functools.partial(spread_kernel, group, digits, lines, more),
+        in_specs=[vmem] * len(grads)
         + [pl.BlockSpec(memory_space=pl.ANY)]
         + [vmem] * more,
         out_specs=[vmem] * outs,
@@ -409,7 +426,7 @@
         ),
         name="spread",
         compiler_params=pltpu.CompilerParams(vmem_limit_bytes=limit << 20),
-    )(index, *grads, factors, *([begun] if more else []))
+    )(*grads, factors, *([begun] if more else []))
 
 
 def exchange(values, axis, size, stride, count):
@@ -431,10 +448,6 @@
     group = min(4, buses)
     depth = buses // group
     block = line_rows // group
-    bus = lax.axis_index("bus")
-    line = lax.axis_index("line")
-    local = jnp.stack([bus % group, line * line_rows]).astype(jnp.int32)
-    order = jnp.stack([bus % group, line]).astype(jnp.int32)
     outage_row = outage_line.reshape(1, outages)
     smem = pl.BlockSpec(memory_space=pltpu.SMEM)
     vmem = pl.BlockSpec(memory_space=pltpu.VMEM)
@@ -448,17 +461,18 @@
         return exchange([mine] * group, "bus", buses, 1, group)
 
     *sent, stacked = partial_flows(
-        injections, factors, group, away, True, local, SEND_LIMIT
+        injections, factors, group, away, True, SEND_LIMIT
     )
-    own = partial_flows(stacked, factors, group, (0,), False, local, 40)
+    own = partial_flows(stacked, factors, group, (0,), False, 40)
     flows = gather_all(reduce_all([*own, *sent]))
-    turned, energy = pl.pallas_call(
+    turned, energy, terms = pl.pallas_call(
         functools.partial(turn_kernel, group),
-        in_specs=[smem, pl.BlockSpec(memory_space=pl.ANY)],
-        out_specs=[vmem] * 2,
+        in_specs=[pl.BlockSpec(memory_space=pl.ANY)],
+        out_specs=[vmem] * 3,
         out_shape=[
             jax.ShapeDtypeStruct((group, outages, block), F32),
             jax.ShapeDtypeStruct((outages, 128), F32),
+            jax.ShapeDtypeStruct((3, group, outages, block), BF16),
         ],
         scratch_shapes=[
             pltpu.VMEM((group, block, outages), F32),
@@ -471,19 +485,19 @@
         ),
         name="turn",
         compiler_params=pltpu.CompilerParams(vmem_limit_bytes=6 << 20),
-    )(local, outage_factors)
+    )(outage_factors)
     picked = pl.pallas_call(
         functools.partial(pick_kernel, group),
-        in_specs=[smem] + [vmem] * (group + 1),
+        in_specs=[vmem] * (group + 1),
         out_specs=vmem,
         out_shape=jax.ShapeDtypeStruct((scen, outages), F32),
         name="pick",
         compiler_params=pltpu.CompilerParams(vmem_limit_bytes=5 << 20),
-    )(local, outage_row, *flows)
+    )(outage_row, *flows)
     picked = exchange([picked] * lines, "line", lines, 1, lines)
     results = pl.pallas_call(
         functools.partial(outage_kernel, group, lines),
-        in_specs=[smem, smem] + [vmem] * (group + lines + 4),
+        in_specs=[smem] + [vmem] * (group + lines + 5),
         out_specs=[vmem] * (group + 1),
         out_shape=[jax.ShapeDtypeStruct((scen, block), F32)] * group
         + [jax.ShapeDtypeStruct((scen + 8, outages), F32)],
@@ -501,22 +515,22 @@
         ],
         name="outage_stage",
         compiler_params=pltpu.CompilerParams(vmem_limit_bytes=11 << 20),
-    )(local, tier, *flows, *picked, turned, energy, table, tier.reshape(1, scen))
+    )(tier, *flows, *picked, turned, energy, terms, table, tier.reshape(1, scen))
     direct, back = results[:group], results[group]
     backs = exchange([back] * lines, "line", lines, 1, lines)
     pieces = pl.pallas_call(
         functools.partial(carry_kernel, group, lines, 2.0 / (outages * buses)),
-        in_specs=[smem] + [vmem] * (group + lines + 1),
+        in_specs=[vmem] * (group + lines + 1),
         out_specs=[vmem] * group,
         out_shape=[jax.ShapeDtypeStruct((scen + 8, block), F32)] * group,
         name="carry",
         compiler_params=pltpu.CompilerParams(vmem_limit_bytes=5 << 20),
-    )(local, outage_row, *direct, *backs)
+    )(outage_row, *direct, *backs)
     total = reduce_all(pieces)
     mean_penalty = total[scen, :scen] / (line_rows * lines * outages * buses)
     grads = gather_all(total[:scen])
-    (begun,) = spread(order, grads[:1], (0,), None, factors, lines, 40)
-    parts = spread(order, grads[1:], away, begun, factors, lines, 40)
+    (begun,) = spread(group, grads[:1], (0,), None, factors, lines, 40)
+    parts = spread(group, grads[1:], away, begun, factors, lines, 40)
     injection_grad = tree_sum(exchange(parts, "line", lines, 1, lines))
     return injection_grad, mean_penalty
 

time: 174 us -> 168 us (0.966)
  Pallas kernels: 112 us -> 106 us
    pallas_call x6, Pallas kernels: 36.5 us -> 33.6 us  [the longest x2 16 us: partial_flows(): pl.pallas_call(functools.partial(flow_kernel, group, digits, fresh), in_s...]
    pallas_call x1, Pallas kernels: 73.6 us -> 71.8 us  [staged(): pl.pallas_call(functools.partial(outage_kernel, group, lines), in_specs=[...]
  transfers between devices with their start and end apart: 21 -> 21, of which waited for: 12 -> 13; matrix products, arithmetic and copies ran while one was open for 0% -> 0% of each run, Pallas kernels for 8% -> 7%
where the time goes in v1:
time: 168 us
  Pallas kernels  106 us (63%)
  waiting for transfers between devices  33.2 us (20%)
  starting transfers between devices  24.8 us (15%)
    pallas_call x1, Pallas kernels, staged(): pl.pallas_call(functools.partial(outage_kernel, group, lines), in_specs=[...  71.8 us
    ppermute x21, waiting for transfers between devices, exchange(): got.append(lax.ppermute(values[j], axis, pairs))  33.2 us
    ppermute x21, starting transfers between devices, exchange(): got.append(lax.ppermute(values[j], axis, pairs))  24.8 us
    pallas_call x2, Pallas kernels, partial_flows(): pl.pallas_call(functools.partial(flow_kernel, group, digits, fresh), in_s...  16 us
    pallas_call x2, Pallas kernels, spread(): pl.pallas_call(functools.partial(spread_kernel, group, digits, lines, mor...  14.9 us
  transfers between devices with their start and end apart: 21, of which 13 were waited for; matrix products, arithmetic and copies ran while one was open for 0% of the time, Pallas kernels for 7%

profile of v1, /device:TPU:0, one launch (start us, length us, event | category | flops | bytes accessed | tf_op | source)
XLA Modules:
  0.0 167.9 jit_solution(17217256848470277420)
XLA Ops:
  0.6 1.2 copy-done.1
  1.9 10.8 %partial_flows.2 = (f32[64,512]{1,0:T(8,128)S(1)}, f32[64,512]{1,0:T(8,128)S(1)}, f32[64,512]{1,0:T(8,128)S(1)}, bf16[128,4352]{1,0:T(8,128)(2,1)S(1)}) custom-call(f32[64,4352]{1,0:T(8,128)S(1)} %copy-done.1, f32[2048,4352]{1,0:T(8,128)} %rest_3_.1), custom_call_target="tpu_custom_call" | custom-call | flops 3422552064 | bytes 26738688 | tf_op jit(solution)/shard_map/partial_flows/pallas_call | solution.py:102
  12.7 3.0 %collective-permute-start = (f32[64,512]{1,0:T(8,128)S(1)}, f32[64,512]{1,0:T(8,128)S(1)}, u32[]{:S(2)}, u32[]{:S(2)}) collective-permute-start(f32[64,512]{1,0:T(8,128)S(1)} %get-tuple-element.21), channel_id=1, source_target_pairs={{0,1},{1,0},{2,3},{3,2},{4,5},{5,4},{6,7},{7,6},{8,9},{9,8},{10,11... | collective-permute-start | bytes 393224 | tf_op jit(solution)/shard_map/ppermute | solution.py:436
  15.7 1.5 collective-permute-start.1
  17.3 5.2 %partial_flows.3 = f32[64,512]{1,0:T(8,128)S(1)} custom-call(bf16[128,4352]{1,0:T(8,128)(2,1)S(1)} %get-tuple-element.20.inj_ref, f32[2048,4352]{1,0:T(8,128)} %rest_3_.1), custom_call_target="tpu_custom_call" | custom-call | flops 1140850688 | bytes 8912896 | tf_op jit(solution)/shard_map/partial_flows/pallas_call | solution.py:102
  22.5 1.0 collective-permute-done.1
  23.5 3.7 %collective-permute-start.5 = (f32[64,512]{1,0:T(8,128)S(1)}, f32[64,512]{1,0:T(8,128)S(1)}, u32[]{:S(2)}, u32[]{:S(2)}) collective-permute-start(f32[64,512]{1,0:T(8,128)S(1)} %add_add_fusion.3), channel_id=1, source_target_pairs={{0,12},{1,13},{2,14},{3,15},{4,8},{5,9},{6,10},{7,11},{8,4},{9,5},... | collective-permute-start | bytes 393224 | tf_op jit(solution)/shard_map/ppermute | solution.py:436
  27.2 0.8 collective-permute-start.3
  28.0 3.6 %collective-permute-done.5 = f32[64,512]{1,0:T(8,128)S(1)} collective-permute-done((f32[64,512]{1,0:T(8,128)S(1)}, f32[64,512]{1,0:T(8,128)S(1)}, u32[]{:S(2)}, u32[]{:S(2)}) %collective-permute-start.5) | collective-permute-done | bytes 131104 | tf_op jit(solution)/shard_map/ppermute | solution.py:436
  31.6 5.4 %collective-permute-done.4 = f32[64,512]{1,0:T(8,128)S(1)} collective-permute-done((f32[64,512]{1,0:T(8,128)S(1)}, f32[64,512]{1,0:T(8,128)S(1)}, u32[]{:S(2)}, u32[]{:S(2)}) %collective-permute-start.4) | collective-permute-done | bytes 131104 | tf_op jit(solution)/shard_map/ppermute | solution.py:436
  37.1 2.4 %collective-permute-start.8 = (f32[64,512]{1,0:T(8,128)S(1)}, f32[64,512]{1,0:T(8,128)S(1)}, u32[]{:S(2)}, u32[]{:S(2)}) collective-permute-start(f32[64,512]{1,0:T(8,128)S(1)} %add_add_fusion.2.rest_0_), channel_id=1, source_target_pairs={{0,3},{1,2},{2,1},{3,0},{4,7},{5,6},{6,5},{7,4},{8,11},{9,10},{10,... | collective-permute-start | bytes 393224 | tf_op jit(solution)/shard_map/ppermute | solution.py:436
  40.6 3.3 %collective-permute-done.8.rest_3_ = f32[64,512]{1,0:T(8,128)S(1)} collective-permute-done((f32[64,512]{1,0:T(8,128)S(1)}, f32[64,512]{1,0:T(8,128)S(1)}, u32[]{:S(2)}, u32[]{:S(2)}) %collective-permute-start.8) | collective-permute-done | bytes 131104 | tf_op jit(solution)/shard_map/ppermute | solution.py:436
  43.9 1.5 collective-permute-done.7.rest_2_
  46.3 2.1 %turn.1 = (f32[4,512,512]{2,1,0:T(8,128)S(1)}, f32[512,128]{1,0:T(8,128)S(1)}, bf16[3,4,512,512]{3,2,1,0:T(8,128)(2,1)S(1)}) custom-call(f32[2048,512]{1,0:T(8,128)S(1)} %copy-done), custom_call_target="tpu_custom_call" | custom-call | flops 2097152 | bytes 12582912 | tf_op jit(solution)/shard_map/turn/pallas_call | solution.py:468
  48.5 71.8 %outage_stage.1 = (f32[64,512]{1,0:T(8,128)S(1)}, f32[64,512]{1,0:T(8,128)S(1)}, f32[64,512]{1,0:T(8,128)S(1)}, f32[64,512]{1,0:T(8,128)S(1)}, f32[72,512]{1,0:T(8,128)S(1)}) custom-call(s32[64]{0:T(128)S(1)} %copy-done.4, f32[64,512]{1,0:T(8,128)S(1)} %add_add_fusion.2.rest_0_, f32[64,512]{1,0:T(8,128)S(1)} %collective-permute-done.6.rest_1_, ...), custom_call_target="tpu_custom_call" | custom-call | tf_op jit(solution)/shard_map/outage_stage/pallas_call | solution.py:498
  120.8 1.0 collective-permute-done.10.rest_5_
  121.8 0.9 carry.1
  122.7 1.3 collective-permute-start.11
  124.0 0.8 collective-permute-start.12
  124.8 1.4 collective-permute-start.13
  126.2 3.2 %collective-permute-done.11 = f32[72,512]{1,0:T(8,128)S(1)} collective-permute-done((f32[72,512]{1,0:T(8,128)S(1)}, f32[72,512]{1,0:T(8,128)S(1)}, u32[]{:S(2)}, u32[]{:S(2)}) %collective-permute-start.11) | collective-permute-done | bytes 147488 | tf_op jit(solution)/shard_map/ppermute | solution.py:436
  129.4 3.5 %collective-permute-done.12 = f32[72,512]{1,0:T(8,128)S(1)} collective-permute-done((f32[72,512]{1,0:T(8,128)S(1)}, f32[72,512]{1,0:T(8,128)S(1)}, u32[]{:S(2)}, u32[]{:S(2)}) %collective-permute-start.12) | collective-permute-done | bytes 147488 | tf_op jit(solution)/shard_map/ppermute | solution.py:436
  133.0 1.8 %collective-permute-start.16 = (f32[72,512]{1,0:T(8,128)S(1)}, f32[72,512]{1,0:T(8,128)S(1)}, u32[]{:S(2)}, u32[]{:S(2)}) collective-permute-start(f32[72,512]{1,0:T(8,128)S(1)} %add_add_fusion.1), channel_id=1, source_target_pairs={{0,12},{1,13},{2,14},{3,15},{4,8},{5,9},{6,10},{7,11},{8,4},{9,5},... | collective-permute-start | bytes 442376 | tf_op jit(solution)/shard_map/ppermute | solution.py:436
  134.9 2.6 %collective-permute-start.14 = (f32[72,512]{1,0:T(8,128)S(1)}, f32[72,512]{1,0:T(8,128)S(1)}, u32[]{:S(2)}, u32[]{:S(2)}) collective-permute-start(f32[72,512]{1,0:T(8,128)S(1)} %add_add_fusion.1), channel_id=1, source_target_pairs={{0,4},{1,5},{2,6},{3,7},{4,0},{5,1},{6,2},{7,3},{8,12},{9,13},{10,... | collective-permute-start | bytes 442376 | tf_op jit(solution)/shard_map/ppermute | solution.py:436
  137.5 4.1 %collective-permute-done.16 = f32[72,512]{1,0:T(8,128)S(1)} collective-permute-done((f32[72,512]{1,0:T(8,128)S(1)}, f32[72,512]{1,0:T(8,128)S(1)}, u32[]{:S(2)}, u32[]{:S(2)}) %collective-permute-start.16) | collective-permute-done | bytes 147488 | tf_op jit(solution)/shard_map/ppermute | solution.py:436
  141.6 4.7 %collective-permute-done.15 = f32[72,512]{1,0:T(8,128)S(1)} collective-permute-done((f32[72,512]{1,0:T(8,128)S(1)}, f32[72,512]{1,0:T(8,128)S(1)}, u32[]{:S(2)}, u32[]{:S(2)}) %collective-permute-start.15) | collective-permute-done | bytes 147488 | tf_op jit(solution)/shard_map/ppermute | solution.py:436
  146.4 1.7 %collective-permute-start.19 = (f32[64,512]{1,0:T(8,128)S(1)}, f32[64,512]{1,0:T(8,128)S(1)}, u32[]{:S(2)}, u32[]{:S(2)}) collective-permute-start(f32[64,512]{1,0:T(8,128)S(1)} %slice.8.rest_0_), channel_id=1, source_target_pairs={{0,3},{1,2},{2,1},{3,0},{4,7},{5,6},{6,5},{7,4},{8,11},{9,10},{10,... | collective-permute-start | bytes 393224 | tf_op jit(solution)/shard_map/ppermute | solution.py:436
  148.9 1.1 collective-permute-start.17
  150.0 5.2 %spread.2.rest_4_ = f32[64,4352]{1,0:T(8,128)S(1)} custom-call(f32[64,512]{1,0:T(8,128)S(1)} %slice.8.rest_0_, f32[2048,4352]{1,0:T(8,128)} %rest_3_.1), custom_call_target="tpu_custom_call" | custom-call | flops 1140850688 | bytes 8912896 | tf_op jit(solution)/shard_map/spread/pallas_call | solution.py:410
  155.3 9.7 %spread.3 = (f32[32,4352]{1,0:T(8,128)S(1)}, f32[32,4352]{1,0:T(8,128)S(1)}) custom-call(f32[64,512]{1,0:T(8,128)S(1)} %collective-permute-done.17.rest_0_, f32[64,512]{1,0:T(8,128)S(1)} %collective-permute-done.18.rest_1_, f32[64,512]{1,0:T(8,128)S(1)} %collective-permute-done.19.rest_2_, f32[2048,4352]{1,0:T(8,128)} %rest_3_.1, f32[64,4352]{1,0:T(8,128)S(1)} %spread.2.rest_4_), custom_call_target="tpu_custom_call" | custom-call | flops 3422552064 | bytes 26738688 | tf_op jit(solution)/shard_map/spread/pallas_call | solution.py:410
  165.6 1.4 collective-permute-done.20
  167.0 0.9 add.51
  (35 shorter events, 4.2 us)
Async XLA Ops:
  0.6 1.2 copy-start.1
  12.7 9.8 %collective-permute-start = (f32[64,512]{1,0:T(8,128)S(1)}, f32[64,512]{1,0:T(8,128)S(1)}, u32[]{:S(2)}, u32[]{:S(2)}) collective-permute-start(f32[64,512]{1,0:T(8,128)S(1)} %get-tuple-element.21), channel_id=1, source_target_pairs={{0,1},{1,0},{2,3},{3,2},{4,5},{5,4},{6,7},{7,6},{8,9},{9,8},{10,11... | collective-permute-start | bytes 393224 | tf_op jit(solution)/shard_map/ppermute | solution.py:436
  15.7 7.8 %collective-permute-start.1 = (f32[64,512]{1,0:T(8,128)S(1)}, f32[64,512]{1,0:T(8,128)S(1)}, u32[]{:S(2)}, u32[]{:S(2)}) collective-permute-start(f32[64,512]{1,0:T(8,128)S(1)} %get-tuple-element.22), channel_id=1, source_target_pairs={{0,2},{1,3},{2,0},{3,1},{4,6},{5,7},{6,4},{7,5},{8,10},{9,11},{10,... | collective-permute-start | bytes 393224 | tf_op jit(solution)/shard_map/ppermute | solution.py:436
  17.2 6.3 %collective-permute-start.2 = (f32[64,512]{1,0:T(8,128)S(1)}, f32[64,512]{1,0:T(8,128)S(1)}, u32[]{:S(2)}, u32[]{:S(2)}) collective-permute-start(f32[64,512]{1,0:T(8,128)S(1)} %get-tuple-element.23), channel_id=1, source_target_pairs={{0,3},{1,2},{2,1},{3,0},{4,7},{5,6},{6,5},{7,4},{8,11},{9,10},{10,... | collective-permute-start | bytes 393224 | tf_op jit(solution)/shard_map/ppermute | solution.py:436
  17.3 28.4 %copy-start.3 = (s32[512]{0:T(512)S(1)}, s32[512]{0:T(512)}, u32[]{:S(2)}) copy-start(s32[512]{0:T(512)} %param.9) | copy-start | bytes 6148
  17.3 29.1 %copy-start = (f32[2048,512]{1,0:T(8,128)S(1)}, f32[2048,512]{1,0:T(8,128)}, u32[]{:S(2)}) copy-start(f32[2048,512]{1,0:T(8,128)} %factor_ref.5) | copy-start | bytes 12582916
  22.5 26.0 %copy-start.2 = (s32[4,2048]{1,0:T(4,128)S(1)}, s32[4,2048]{1,0:T(4,128)}, u32[]{:S(2)}) copy-start(s32[4,2048]{1,0:T(4,128)} %rest_9_.1) | copy-start | bytes 98308
  22.5 26.0 %copy-start.4 = (s32[64]{0:T(128)S(1)}, s32[64]{0:T(128)}, u32[]{:S(2)}) copy-start(s32[64]{0:T(128)} %tier_ref.1) | copy-start | bytes 772
  23.5 8.1 %collective-permute-start.5 = (f32[64,512]{1,0:T(8,128)S(1)}, f32[64,512]{1,0:T(8,128)S(1)}, u32[]{:S(2)}, u32[]{:S(2)}) collective-permute-start(f32[64,512]{1,0:T(8,128)S(1)} %add_add_fusion.3), channel_id=1, source_target_pairs={{0,12},{1,13},{2,14},{3,15},{4,8},{5,9},{6,10},{7,11},{8,4},{9,5},... | collective-permute-start | bytes 393224 | tf_op jit(solution)/shard_map/ppermute | solution.py:436
  27.2 9.8 %collective-permute-start.4 = (f32[64,512]{1,0:T(8,128)S(1)}, f32[64,512]{1,0:T(8,128)S(1)}, u32[]{:S(2)}, u32[]{:S(2)}) collective-permute-start(f32[64,512]{1,0:T(8,128)S(1)} %add_add_fusion.3), channel_id=1, source_target_pairs={{0,8},{1,9},{2,10},{3,11},{4,12},{5,13},{6,14},{7,15},{8,0},{9,1},... | collective-permute-start | bytes 393224 | tf_op jit(solution)/shard_map/ppermute | solution.py:436
  27.2 9.8 %collective-permute-start.3 = (f32[64,512]{1,0:T(8,128)S(1)}, f32[64,512]{1,0:T(8,128)S(1)}, u32[]{:S(2)}, u32[]{:S(2)}) collective-permute-start(f32[64,512]{1,0:T(8,128)S(1)} %add_add_fusion.3), channel_id=1, source_target_pairs={{0,4},{1,5},{2,6},{3,7},{4,0},{5,1},{6,2},{7,3},{8,12},{9,13},{10,... | collective-permute-start | bytes 393224 | tf_op jit(solution)/shard_map/ppermute | solution.py:436
  37.1 6.8 %collective-permute-start.8 = (f32[64,512]{1,0:T(8,128)S(1)}, f32[64,512]{1,0:T(8,128)S(1)}, u32[]{:S(2)}, u32[]{:S(2)}) collective-permute-start(f32[64,512]{1,0:T(8,128)S(1)} %add_add_fusion.2.rest_0_), channel_id=1, source_target_pairs={{0,3},{1,2},{2,1},{3,0},{4,7},{5,6},{6,5},{7,4},{8,11},{9,10},{10,... | collective-permute-start | bytes 393224 | tf_op jit(solution)/shard_map/ppermute | solution.py:436
  39.5 6.0 %collective-permute-start.7 = (f32[64,512]{1,0:T(8,128)S(1)}, f32[64,512]{1,0:T(8,128)S(1)}, u32[]{:S(2)}, u32[]{:S(2)}) collective-permute-start(f32[64,512]{1,0:T(8,128)S(1)} %add_add_fusion.2.rest_0_), channel_id=1, source_target_pairs={{0,2},{1,3},{2,0},{3,1},{4,6},{5,7},{6,4},{7,5},{8,10},{9,11},{10,... | collective-permute-start | bytes 393224 | tf_op jit(solution)/shard_map/ppermute | solution.py:436
  40.2 5.4 %collective-permute-start.6 = (f32[64,512]{1,0:T(8,128)S(1)}, f32[64,512]{1,0:T(8,128)S(1)}, u32[]{:S(2)}, u32[]{:S(2)}) collective-permute-start(f32[64,512]{1,0:T(8,128)S(1)} %add_add_fusion.2.rest_0_), channel_id=1, source_target_pairs={{0,1},{1,0},{2,3},{3,2},{4,5},{5,4},{6,7},{7,6},{8,9},{9,8},{10,11... | collective-permute-start | bytes 393224 | tf_op jit(solution)/shard_map/ppermute | solution.py:436
  46.2 2.2 %collective-permute-start.9 = (f32[64,512]{1,0:T(8,128)S(1)}, f32[64,512]{1,0:T(8,128)S(1)}, u32[]{:S(2)}, u32[]{:S(2)}) collective-permute-start(f32[64,512]{1,0:T(8,128)S(1)} %pick.1.rest_4_), channel_id=1, source_target_pairs={{0,16},{16,0},{1,17},{17,1},{2,18},{18,2},{3,19},{19,3},{4,20},{20... | collective-permute-start | bytes 393224 | tf_op jit(solution)/shard_map/ppermute | solution.py:436
  120.3 1.5 collective-permute-start.10
  122.7 6.8 %collective-permute-start.11 = (f32[72,512]{1,0:T(8,128)S(1)}, f32[72,512]{1,0:T(8,128)S(1)}, u32[]{:S(2)}, u32[]{:S(2)}) collective-permute-start(f32[72,512]{1,0:T(8,128)S(1)} %get-tuple-element.33), channel_id=1, source_target_pairs={{0,1},{1,0},{2,3},{3,2},{4,5},{5,4},{6,7},{7,6},{8,9},{9,8},{10,11... | collective-permute-start | bytes 442376 | tf_op jit(solution)/shard_map/ppermute | solution.py:436
  124.0 9.0 %collective-permute-start.12 = (f32[72,512]{1,0:T(8,128)S(1)}, f32[72,512]{1,0:T(8,128)S(1)}, u32[]{:S(2)}, u32[]{:S(2)}) collective-permute-start(f32[72,512]{1,0:T(8,128)S(1)} %get-tuple-element.34), channel_id=1, source_target_pairs={{0,2},{1,3},{2,0},{3,1},{4,6},{5,7},{6,4},{7,5},{8,10},{9,11},{10,... | collective-permute-start | bytes 442376 | tf_op jit(solution)/shard_map/ppermute | solution.py:436
  124.8 8.1 %collective-permute-start.13 = (f32[72,512]{1,0:T(8,128)S(1)}, f32[72,512]{1,0:T(8,128)S(1)}, u32[]{:S(2)}, u32[]{:S(2)}) collective-permute-start(f32[72,512]{1,0:T(8,128)S(1)} %get-tuple-element.35), channel_id=1, source_target_pairs={{0,3},{1,2},{2,1},{3,0},{4,7},{5,6},{6,5},{7,4},{8,11},{9,10},{10,... | collective-permute-start | bytes 442376 | tf_op jit(solution)/shard_map/ppermute | solution.py:436
  133.0 8.6 %collective-permute-start.16 = (f32[72,512]{1,0:T(8,128)S(1)}, f32[72,512]{1,0:T(8,128)S(1)}, u32[]{:S(2)}, u32[]{:S(2)}) collective-permute-start(f32[72,512]{1,0:T(8,128)S(1)} %add_add_fusion.1), channel_id=1, source_target_pairs={{0,12},{1,13},{2,14},{3,15},{4,8},{5,9},{6,10},{7,11},{8,4},{9,5},... | collective-permute-start | bytes 442376 | tf_op jit(solution)/shard_map/ppermute | solution.py:436
  134.9 11.5 %collective-permute-start.15 = (f32[72,512]{1,0:T(8,128)S(1)}, f32[72,512]{1,0:T(8,128)S(1)}, u32[]{:S(2)}, u32[]{:S(2)}) collective-permute-start(f32[72,512]{1,0:T(8,128)S(1)} %add_add_fusion.1), channel_id=1, source_target_pairs={{0,8},{1,9},{2,10},{3,11},{4,12},{5,13},{6,14},{7,15},{8,0},{9,1},... | collective-permute-start | bytes 442376 | tf_op jit(solution)/shard_map/ppermute | solution.py:436
  134.9 11.5 %collective-permute-start.14 = (f32[72,512]{1,0:T(8,128)S(1)}, f32[72,512]{1,0:T(8,128)S(1)}, u32[]{:S(2)}, u32[]{:S(2)}) collective-permute-start(f32[72,512]{1,0:T(8,128)S(1)} %add_add_fusion.1), channel_id=1, source_target_pairs={{0,4},{1,5},{2,6},{3,7},{4,0},{5,1},{6,2},{7,3},{8,12},{9,13},{10,... | collective-permute-start | bytes 442376 | tf_op jit(solution)/shard_map/ppermute | solution.py:436
  146.4 8.8 %collective-permute-start.19 = (f32[64,512]{1,0:T(8,128)S(1)}, f32[64,512]{1,0:T(8,128)S(1)}, u32[]{:S(2)}, u32[]{:S(2)}) collective-permute-start(f32[64,512]{1,0:T(8,128)S(1)} %slice.8.rest_0_), channel_id=1, source_target_pairs={{0,3},{1,2},{2,1},{3,0},{4,7},{5,6},{6,5},{7,4},{8,11},{9,10},{10,... | collective-permute-start | bytes 393224 | tf_op jit(solution)/shard_map/ppermute | solution.py:436
  148.1 7.2 %collective-permute-start.18 = (f32[64,512]{1,0:T(8,128)S(1)}, f32[64,512]{1,0:T(8,128)S(1)}, u32[]{:S(2)}, u32[]{:S(2)}) collective-permute-start(f32[64,512]{1,0:T(8,128)S(1)} %slice.8.rest_0_), channel_id=1, source_target_pairs={{0,2},{1,3},{2,0},{3,1},{4,6},{5,7},{6,4},{7,5},{8,10},{9,11},{10,... | collective-permute-start | bytes 393224 | tf_op jit(solution)/shard_map/ppermute | solution.py:436
  148.9 6.4 %collective-permute-start.17 = (f32[64,512]{1,0:T(8,128)S(1)}, f32[64,512]{1,0:T(8,128)S(1)}, u32[]{:S(2)}, u32[]{:S(2)}) collective-permute-start(f32[64,512]{1,0:T(8,128)S(1)} %slice.8.rest_0_), channel_id=1, source_target_pairs={{0,1},{1,0},{2,3},{3,2},{4,5},{5,4},{6,7},{7,6},{8,9},{9,8},{10,11... | collective-permute-start | bytes 393224 | tf_op jit(solution)/shard_map/ppermute | solution.py:436
  165.0 2.0 %collective-permute-start.20 = (f32[32,4352]{1,0:T(8,128)S(1)}, f32[32,4352]{1,0:T(8,128)S(1)}, u32[]{:S(2)}, u32[]{:S(2)}) collective-permute-start(f32[32,4352]{1,0:T(8,128)S(1)} %get-tuple-element.37), channel_id=1, source_target_pairs={{0,16},{16,0},{1,17},{17,1},{2,18},{18,2},{3,19},{19,3},{4,20},{20... | collective-permute-start | bytes 1671176 | tf_op jit(solution)/shard_map/ppermute | solution.py:436
